TPU v7x, 32 devices: a whole 2x2x4 slice. The times are simulated.
32 devices in a mesh: groups: 2 (over x), frame: 16 (over z, y, core).
Axes of the slice: x: 2, y: 2, z: 4, core: 2. Of those that a mesh axis runs over, the one named last changes fastest.
Arguments:
- latent: bfloat16 [128, 32, 1152], P(('groups', 'frame')), parts along dimension 0, may hold values from -6 to 6
- ln_gain: float32 [1152], replicated, may hold values from 0.1 to 1.9
- q_gain: float32 [72], replicated, may hold values from 0.1 to 1.9
- k_gain: float32 [72], replicated, may hold values from 0.1 to 1.9
- w_qkv: bfloat16 [1152, 3456], replicated, may hold values from -0.1875 to 0.1875
- w_out: bfloat16 [1152, 1152], replicated, may hold values from -0.5 to 0.5
Outputs:
- result: bfloat16 [128, 32, 1152], P(('groups', 'frame')), parts along dimension 0
There are 2 independent parts, one for each index of `groups`. A program takes and returns all parts, laid end to end along the dimension named above; an argument that names none is the same for every part. Nothing has to cross between parts.
All inputs are finite; a program needn't handle non-finite values.
Results may differ from a plain program's by a relative error of at most 0.006.
Values may be sent and summed in bfloat16 or wider, within the bound.
A program may use at most 64 MiB of HBM per device.

v0:
```python
import jax
import jax.numpy as jnp
from jax import lax
from jax.sharding import PartitionSpec as P

HEADS = 16
HEAD_DIM = 72


def layer_norm(rows, ln_gain):
    values = rows.astype(jnp.float32)
    center = values - jnp.mean(values, axis=-1, keepdims=True)
    spread = jnp.mean(center * center, axis=-1, keepdims=True)
    return (center * lax.rsqrt(spread + 1e-06) * ln_gain).astype(jnp.bfloat16)


def head_norm(values, gain):
    shaped = values.reshape(values.shape[:-1] + (HEADS, HEAD_DIM))
    mean_sq = jnp.mean(shaped * shaped, axis=-1, keepdims=True)
    return (shaped * lax.rsqrt(mean_sq + 1e-06) * gain).astype(jnp.bfloat16).reshape(values.shape)


def project(normed, w_qkv, q_gain, k_gain):
    width = normed.shape[-1]
    mixed = jnp.dot(normed.reshape(-1, width), w_qkv, preferred_element_type=jnp.float32)
    mixed = mixed.reshape(normed.shape[:-1] + (3 * width,))
    query = head_norm(mixed[..., :width], q_gain)
    keys = head_norm(mixed[..., width : 2 * width], k_gain)
    values = mixed[..., 2 * width :].astype(jnp.bfloat16)
    return (query, keys, values)


def attend(query, keys, values):
    lead = query.shape[0]
    others = query.shape[1]
    q_four = query.reshape(lead, others, HEADS, HEAD_DIM)
    k_four = keys.reshape(lead, others, HEADS, HEAD_DIM)
    v_four = values.reshape(lead, others, HEADS, HEAD_DIM)
    scores = jnp.einsum(
        "tshe,ushe->shtu", q_four, k_four, preferred_element_type=jnp.float32
    ) * HEAD_DIM ** (-0.5)
    weights = jnp.exp(scores)
    weights = (weights / jnp.sum(weights, axis=-1, keepdims=True)).astype(jnp.bfloat16)
    mixed = jnp.einsum("shtu,ushe->tshe", weights, v_four, preferred_element_type=jnp.float32)
    return mixed.astype(jnp.bfloat16).reshape(query.shape)


def body(latent, ln_gain, q_gain, k_gain, w_qkv, w_out):
    device_count = lax.axis_size("frame")
    rows, columns, model = latent.shape
    positions = rows * columns
    per_peer = positions // device_count
    flat = latent.reshape(positions, model)
    normed = layer_norm(flat, ln_gain)
    query, keys, values = project(
        lax.all_to_all(
            normed.reshape(device_count, per_peer, model),
            "frame",
            split_axis=0,
            concat_axis=0,
            tiled=True,
        ),
        w_qkv,
        q_gain,
        k_gain,
    )
    mixed = attend(query, keys, values)
    returned = lax.all_to_all(mixed, "frame", split_axis=0, concat_axis=0, tiled=True)
    attended = returned.reshape(positions, model)
    branch = jnp.dot(attended, w_out, preferred_element_type=jnp.float32)
    result = flat.astype(jnp.float32) + branch
    return result.astype(jnp.bfloat16).reshape(latent.shape)


def solution(mesh):
    placed = (P(("groups", "frame"), None, None), P(), P(), P(), P(), P())
    return jax.shard_map(
        body,
        mesh=mesh,
        in_specs=placed,
        out_specs=P(("groups", "frame"), None, None),
        check_vma=False,
    )
```

profile of v0, /device:TPU:0, one launch (start us, length us, event | category | flops | bytes accessed | tf_op | source)
XLA Modules:
  0.0 63.9 jit_solution(6574092277274631922)
XLA Ops:
  0.0 0.0 copy-start
  0.0 1.2 %convert_reduce_fusion = f32[4,32]{1,0:T(4,128)S(1)} fusion(bf16[4,32,1152]{2,1,0:T(8,128)(2,1)} %param.6), kind=kLoop, calls=%fused_computation.21 | loop fusion | flops 294784 | bytes 295424 | tf_op jit(solution)/shard_map/reduce_sum | solution.py:12
  1.2 1.2 %multiply_reduce_fusion.2 = f32[4,32]{1,0:T(4,128)S(1)} fusion(bf16[4,32,1152]{2,1,0:T(8,128)(2,1)} %param.6, f32[4,32]{1,0:T(4,128)S(1)} %broadcast_multiply_fusion), kind=kLoop, calls=%fused_computation.15 | loop fusion | flops 589696 | bytes 295936 | tf_op jit(solution)/shard_map/reduce_sum | solution.py:13
  2.4 0.1 div.23
  2.5 1.0 %convert_element_type.52 = f32[4,32,1152]{2,1,0:T(8,128)S(1)} convert(bf16[4,32,1152]{2,1,0:T(8,128)(2,1)} %param.6) | non-fusion elementwise | flops 147456 | bytes 884736 | tf_op jit(solution)/shard_map/convert_element_type | solution.py:71
  3.5 0.1 rsqrt.28
  3.6 0.8 %multiply_convert_fusion.2 = bf16[16,8,1152]{2,1,0:T(8,128)(2,1)S(1)} fusion(f32[16,8,1152]{2,1,0:T(8,128)S(1)} %bitcast.16, f32[1152]{0:T(1024)} %param.7, f32[16,8]{1,0:T(8,128)S(1)} %rsqrt.28, f32[16,8]{1,0:T(8,128)S(1)} %div.23), kind=kLoop, calls=%fused_computation.14 | loop fusion | flops 589824 | bytes 890368 | tf_op jit(solution)/shard_map/convert_element_type | solution.py:14
  4.5 17.8 %all_to_all.10 = bf16[16,8,1152]{2,1,0:T(8,128)(2,1)S(1)} all-to-all(bf16[16,8,1152]{2,1,0:T(8,128)(2,1)S(1)} %multiply_convert_fusion.2), channel_id=1, replica_groups=mesh['groups'=2,'frame'=16] {'frame'}, dimensions={0} | all-to-all | bytes 589824 | tf_op jit(solution)/shard_map/all_to_all | solution.py:56
  22.2 4.6 %fusion = f32[16,8,3456]{2,1,0:T(8,128)S(1)} fusion(bf16[16,8,1152]{2,1,0:T(8,128)(2,1)S(1)} %all_to_all.10, bf16[1152,3456]{1,0:T(8,128)(2,1)} %param.10), kind=kOutput, calls=%fused_computation | convolution fusion | flops 1019215872 | bytes 10027008 | tf_op jit(solution)/shard_map/dot_general | solution.py:25
  26.9 1.1 %fusion.18 = (f32[16,8,1152]{2,1,0:T(8,128)}, f32[16,8,1152]{2,1,0:T(8,128)}) fusion(f32[16,8,3456]{2,1,0:T(8,128)S(1)} %fusion), kind=kLoop, calls=%fused_computation.29 | loop fusion | bytes 2359296 | tf_op jit(solution)/shard_map/slice | solution.py:27
  28.0 1.8 %reshape.96 = bf16[16,8,16,72]{3,2,1,0:T(8,128)(2,1)} reshape(bf16[16,8,1152]{2,1,0:T(8,128)(2,1)S(1)} %slice.17) | data formatting | bytes 589824 | tf_op jit(solution)/shard_map/reshape | solution.py:38
  29.7 0.0 copy-start.1
  29.7 0.0 copy-start.2
  29.7 2.9 %reshape.97 = f32[16,8,16,72]{3,2,1,0:T(8,128)} reshape(f32[16,8,1152]{2,1,0:T(8,128)} %get-tuple-element.5) | data formatting | bytes 1179648 | tf_op jit(solution)/shard_map/reshape | solution.py:18
  32.7 1.6 %multiply_reduce_fusion.1 = f32[16,8,16]{2,1,0:T(8,128)S(1)} fusion(f32[16,8,16,72]{3,2,1,0:T(8,128)} %reshape.97), kind=kLoop, calls=%fused_computation.12 | loop fusion | flops 292864 | bytes 598016 | tf_op jit(solution)/shard_map/reduce_sum | solution.py:19
  34.3 3.0 %reshape.98 = f32[16,8,16,72]{3,2,1,0:T(8,128)} reshape(f32[16,8,1152]{2,1,0:T(8,128)} %get-tuple-element.6) | data formatting | bytes 1179648 | tf_op jit(solution)/shard_map/reshape | solution.py:18
  37.3 1.6 %multiply_reduce_fusion = f32[16,8,16]{2,1,0:T(8,128)S(1)} fusion(f32[16,8,16,72]{3,2,1,0:T(8,128)} %reshape.98), kind=kLoop, calls=%fused_computation.10 | loop fusion | flops 292864 | bytes 598016 | tf_op jit(solution)/shard_map/reduce_sum | solution.py:19
  38.9 0.0 copy-done.1
  38.9 0.0 copy-done.2
  38.9 1.9 %multiply_convert_fusion = (bf16[16,8,16,72]{3,2,1,0:T(8,128)(2,1)S(1)}, bf16[16,8,16,72]{3,2,1,0:T(8,128)(2,1)S(1)}) fusion(f32[16,8,16,72]{3,2,1,0:T(8,128)} %reshape.98, f32[72]{0:T(128)S(1)} %copy-done.1, f32[16,8,16]{2,1,0:T(8,128)S(1)} %add_rsqrt_fusion, f32[72]{0:T(128)S(1)} %copy-done.2, f32[16,8,16,72]{3,2,1,0:T(8,128)} %reshape.97, ...), kind=kLoop, calls=%fused_computation.9 | loop fusion | flops 884736 | bytes 1786432 | tf_op jit(solution)/shard_map/convert_element_type | solution.py:20
  40.8 1.8 %fusion.3 = f32[8,16,16,16]{2,3,1,0:T(8,128)} fusion(bf16[16,8,16,72]{3,2,1,0:T(8,128)(2,1)S(1)} %get-tuple-element.7, bf16[16,8,16,72]{3,2,1,0:T(8,128)(2,1)S(1)} %get-tuple-element.8), kind=kOutput, calls=%fused_computation.5 | convolution fusion | flops 4751360 | bytes 720896 | tf_op jit(solution)/shard_map/tshe,ushe->shtu/dot_general | solution.py:39
  42.6 3.1 %fusion.4 = bf16[16,8,16,72]{3,0,2,1:T(8,128)(2,1)} fusion(f32[8,16,16,16]{2,3,1,0:T(8,128)} %fusion.3, bf16[16,8,16,72]{3,2,1,0:T(8,128)(2,1)} %reshape.96), kind=kOutput, calls=%fused_computation.7 | convolution fusion | flops 4933647 | bytes 720896 | tf_op jit(solution)/shard_map/shtu,ushe->tshe/dot_general | solution.py:44
  45.7 2.0 %copy.20 = bf16[16,8,16,72]{3,2,1,0:T(8,128)(2,1)} copy(bf16[16,8,16,72]{3,0,2,1:T(8,128)(2,1)} %fusion.4) | data formatting | bytes 589824 | tf_op jit(solution)/shard_map/convert_element_type | solution.py:45
  47.7 1.5 %reshape.99 = bf16[16,8,1152]{2,1,0:T(8,128)(2,1)S(1)} reshape(bf16[16,8,16,72]{3,2,1,0:T(8,128)(2,1)} %copy.20) | data formatting | bytes 589824 | tf_op jit(solution)/shard_map/reshape | solution.py:45
  49.2 13.3 %all_to_all.11 = bf16[16,8,1152]{2,1,0:T(8,128)(2,1)S(1)} all-to-all(bf16[16,8,1152]{2,1,0:T(8,128)(2,1)S(1)} %reshape.99), channel_id=1, replica_groups=mesh['groups'=2,'frame'=16] {'frame'}, dimensions={0} | all-to-all | bytes 589824 | tf_op jit(solution)/shard_map/all_to_all | solution.py:68
  62.6 0.0 copy-done
  62.6 1.3 %fusion.2 = bf16[128,1152]{1,0:T(8,128)(2,1)} fusion(f32[128,1152]{1,0:T(8,128)S(1)} %bitcast.17, bf16[1152,1152]{1,0:T(8,128)(2,1)S(1)} %copy-done, bf16[16,8,1152]{2,1,0:T(8,128)(2,1)S(1)} %all_to_all.11), kind=kOutput, calls=%fused_computation.3 | convolution fusion | flops 340033536 | bytes 3833856 | tf_op jit(solution)/shard_map/dot_general | solution.py:70
  (5 shorter events, 0.1 us)
Async XLA Ops:
  0.0 62.6 %copy-start = (bf16[1152,1152]{1,0:T(8,128)(2,1)S(1)}, bf16[1152,1152]{1,0:T(8,128)(2,1)}, u32[]{:S(2)}) copy-start(bf16[1152,1152]{1,0:T(8,128)(2,1)} %param.11) | copy-start | bytes 7962628
  29.7 9.1 %copy-start.1 = (f32[72]{0:T(128)S(1)}, f32[72]{0:T(128)}, u32[]{:S(2)}) copy-start(f32[72]{0:T(128)} %param.9) | copy-start | bytes 868
  29.7 9.1 %copy-start.2 = (f32[72]{0:T(128)S(1)}, f32[72]{0:T(128)}, u32[]{:S(2)}) copy-start(f32[72]{0:T(128)} %param.8) | copy-start | bytes 868
where the time goes:
time: 64.5 us; the launch traced here: 63.9 us
  blocking collectives  31.1 us (48%)
  local copies, waits for them, and re-layouts  12.5 us (19%)
  matrix products  10.8 us (17%)
  other arithmetic  9.38 us (15%)
    all_to_all x1, blocking collectives, body(): lax.all_to_all(normed.reshape(device_count, per_peer, model), 'frame', sp...  17.8 us
    all_to_all x1, blocking collectives, body(): lax.all_to_all(mixed, 'frame', split_axis=0, concat_axis=0, tiled=True)  13.3 us
    reshape x2, local copies, waits for them, and re-layouts, head_norm(): shaped = values.reshape(values.shape[:-1] + (HEADS, HEAD_DIM))  5.91 us
    dot_general x1, matrix products, project(): jnp.dot(normed.reshape(-1, width), w_qkv, preferred_element_type=jnp.floa...  4.61 us
    reduce_sum x2, other arithmetic, head_norm(): mean_sq = jnp.mean(shaped * shaped, axis=-1, keepdims=True)  3.14 us
    dot_general x1, matrix products, attend(): jnp.einsum('shtu,ushe->tshe', weights, v_four, preferred_element_type=jnp...  3.11 us
    convert_element_type x1, local copies, waits for them, and re-layouts, attend(): return mixed.astype(jnp.bfloat16).reshape(query.shape)  1.97 us
    convert_element_type x1, other arithmetic, head_norm(): (shaped * lax.rsqrt(mean_sq + 1e-06) * gain).astype(jnp.bfloat16)  1.92 us

commit v1 on v0

--- a/solution.py
+++ b/solution.py
@@ -1,10 +1,270 @@
+import functools
+
 import jax
 import jax.numpy as jnp
 from jax import lax
+from jax.experimental import pallas as pl
+from jax.experimental.pallas import tpu as pltpu
 from jax.sharding import PartitionSpec as P
 
 HEADS = 16
 HEAD_DIM = 72
+LANES = 128
+IN_CUTS = (0, 512, 1024, 1152)
+OUT_CUTS = (0, 256, 768, 1152)
+MESH = pl.DeviceIdType.MESH
+F32 = jnp.float32
+BF16 = jnp.bfloat16
+
+
+def split_dot(values, ones):
+    high = values.astype(BF16)
+    low = (values - high.astype(F32)).astype(BF16)
+    return jnp.dot(high, ones, preferred_element_type=F32) + jnp.dot(
+        low, ones, preferred_element_type=F32
+    )
+
+
+def kernel(
+    n,
+    lat_ref,
+    ln_ref,
+    qg_ref,
+    kg_ref,
+    wq_hbm,
+    wo_hbm,
+    out_ref,
+    xs,
+    xr,
+    ys,
+    yr,
+    wq,
+    wo,
+    acc,
+    qn,
+    kn,
+    vb,
+    wq_sem,
+    wo_sem,
+    s1,
+    r1,
+    s2,
+    r2,
+):
+    rows, columns, model = lat_ref.shape
+    tokens = rows * columns
+    per = tokens // n
+    me = lax.axis_index("frame")
+    in_parts = list(zip(IN_CUTS[:-1], IN_CUTS[1:]))
+    out_parts = list(zip(OUT_CUTS[:-1], OUT_CUTS[1:]))
+
+    barrier = pltpu.get_barrier_semaphore()
+
+    def greet(k, _):
+        pl.semaphore_signal(
+            barrier, inc=1, device_id={"frame": lax.rem(me + k, n)}, device_id_type=MESH
+        )
+        return 0
+
+    lax.fori_loop(1, n, greet, 0)
+
+    loads = []
+    for c, (a, b) in enumerate(in_parts):
+        loads.append(
+            pltpu.make_async_copy(wq_hbm.at[pl.ds(a, b - a)], wq.at[pl.ds(a, b - a)], wq_sem.at[c])
+        )
+        loads[-1].start()
+    load_out = pltpu.make_async_copy(wo_hbm, wo, wo_sem)
+    load_out.start()
+
+    values = lat_ref[...].astype(F32).reshape(tokens, model)
+    center = values - jnp.mean(values, axis=-1, keepdims=True)
+    spread = jnp.mean(center * center, axis=-1, keepdims=True)
+    normed = center * lax.rsqrt(spread + 1e-06) * ln_ref[...]
+    xs[...] = normed.reshape(n, per, model).astype(BF16)
+    xr[pl.ds(me, 1)] = xs[pl.ds(me, 1)]
+
+    pl.semaphore_wait(barrier, n - 1)
+
+    def copy(src, dst, send, recv, c, a, b, k, to, slot):
+        return pltpu.make_async_remote_copy(
+            src_ref=src.at[to, :, pl.ds(a, b - a)],
+            dst_ref=dst.at[slot, :, pl.ds(a, b - a)],
+            send_sem=send.at[c, k],
+            recv_sem=recv.at[c, k],
+            device_id={"frame": to},
+            device_id_type=MESH,
+        )
+
+    def send_all(src, dst, send, recv, c, a, b):
+        def one(k, _):
+            copy(src, dst, send, recv, c, a, b, k, lax.rem(me + k, n), me).start()
+            return 0
+
+        lax.fori_loop(1, n, one, 0)
+
+    def wait_recv_all(src, dst, send, recv, c, a, b):
+        def one(k, _):
+            copy(
+                src, dst, send, recv, c, a, b, k, lax.rem(me + k, n), lax.rem(me + n - k, n)
+            ).wait_recv()
+            return 0
+
+        lax.fori_loop(1, n, one, 0)
+
+    def wait_send_all(src, dst, send, recv, c, a, b):
+        def one(k, _):
+            copy(src, dst, send, recv, c, a, b, k, lax.rem(me + k, n), me).wait_send()
+            return 0
+
+        lax.fori_loop(1, n, one, 0)
+
+    for c, (a, b) in enumerate(in_parts):
+        send_all(xs, xr, s1, r1, c, a, b)
+
+    lane = lax.broadcasted_iota(jnp.int32, (model, LANES), 0)
+    head = lax.broadcasted_iota(jnp.int32, (model, LANES), 1)
+    gather = ((lane >= head * HEAD_DIM) & (lane < (head + 1) * HEAD_DIM)).astype(F32).astype(BF16)
+    head_t = lax.broadcasted_iota(jnp.int32, (LANES, model), 0)
+    lane_t = lax.broadcasted_iota(jnp.int32, (LANES, model), 1)
+    inside = (lane_t >= head_t * HEAD_DIM) & (lane_t < (head_t + 1) * HEAD_DIM)
+    spread_t = inside.astype(F32).astype(BF16)
+    entry = lax.broadcasted_iota(jnp.int32, (HEAD_DIM, model), 0)
+    place = lax.broadcasted_iota(jnp.int32, (HEAD_DIM, model), 1)
+    picked = entry == place
+    for h in range(1, HEADS):
+        picked = picked | (entry + h * HEAD_DIM == place)
+    repeat = picked.astype(F32)
+
+    def whole_gain(ref):
+        rows8 = jnp.broadcast_to(ref[...], (8, HEAD_DIM))
+        return jnp.dot(
+            rows8, repeat, preferred_element_type=F32, precision=lax.Precision.HIGHEST
+        )[0:1]
+
+    q_gain = whole_gain(qg_ref)
+    k_gain = whole_gain(kg_ref)
+
+    width = 3 * model
+    step = model // 3
+    for c, (a, b) in enumerate(in_parts):
+        wait_recv_all(xs, xr, s1, r1, c, a, b)
+        loads[c].wait()
+        part = xr[:, :, a:b].astype(F32).reshape(tokens, b - a).astype(BF16)
+        for col in range(0, width, step):
+            product = jnp.dot(part, wq[a:b, col : col + step], preferred_element_type=F32)
+            if c == 0:
+                acc[:, col : col + step] = product
+            else:
+                acc[:, col : col + step] += product
+
+    def head_norm(block, gain):
+        sums = split_dot(block * block, gather)
+        scale = lax.rsqrt(sums * (1.0 / HEAD_DIM) + 1e-06)
+        return (block * split_dot(scale, spread_t) * gain).astype(BF16)
+
+    qn[...] = head_norm(acc[:, :model], q_gain)
+    kn[...] = head_norm(acc[:, model : 2 * model], k_gain)
+    vb[...] = acc[:, 2 * model :].astype(BF16)
+
+    row_i = lax.broadcasted_iota(jnp.int32, (tokens, tokens), 0)
+    col_i = lax.broadcasted_iota(jnp.int32, (tokens, tokens), 1)
+    same = lax.rem(row_i, per) == lax.rem(col_i, per)
+
+    def head_mask(h, lo, hi):
+        at = lax.broadcasted_iota(jnp.int32, (tokens, hi - lo), 1) + lo
+        return (at >= h * HEAD_DIM) & (at < (h + 1) * HEAD_DIM)
+
+    probs = {}
+
+    def attend(h):
+        lo = h * HEAD_DIM // LANES * LANES
+        hi = -(-(h + 1) * HEAD_DIM // LANES) * LANES
+        mask = head_mask(h, lo, hi)
+        query = jnp.where(mask, qn[:, lo:hi].astype(F32), 0.0).astype(BF16)
+        scores = lax.dot_general(
+            query, kn[:, lo:hi], (((1,), (1,)), ((), ())), preferred_element_type=F32
+        ) * (HEAD_DIM**-0.5)
+        weights = jnp.where(same, jnp.exp(scores), 0.0)
+        total = jnp.sum(weights, axis=-1, keepdims=True)
+        probs[h] = (weights * (1.0 / total)).astype(BF16)
+
+    for c, (a, b) in enumerate(out_parts):
+        for tile in range(a, b, LANES):
+            out_tile = None
+            for h in range(tile // HEAD_DIM, (tile + LANES - 1) // HEAD_DIM + 1):
+                if h not in probs:
+                    attend(h)
+                mask = head_mask(h, tile, tile + LANES)
+                value = jnp.where(mask, vb[:, tile : tile + LANES].astype(F32), 0.0).astype(BF16)
+                term = jnp.dot(probs[h], value, preferred_element_type=F32)
+                out_tile = term if out_tile is None else out_tile + term
+            ys[:, :, tile : tile + LANES] = out_tile.reshape(n, per, LANES).astype(BF16)
+        send_all(ys, yr, s2, r2, c, a, b)
+    yr[pl.ds(me, 1)] = ys[pl.ds(me, 1)]
+
+    load_out.wait()
+    branch = lat_ref[...].astype(F32).reshape(tokens, model)
+    for c, (a, b) in enumerate(out_parts):
+        wait_recv_all(ys, yr, s2, r2, c, a, b)
+        part = yr[:, :, a:b].astype(F32).reshape(tokens, b - a).astype(BF16)
+        product = jnp.dot(part, wo[a:b, :], preferred_element_type=F32)
+        if c == 0:
+            acc[:, :model] = product
+        elif c < len(out_parts) - 1:
+            acc[:, :model] += product
+        else:
+            product = acc[:, :model] + product
+            out_ref[...] = (branch + product).reshape(rows, columns, model).astype(BF16)
+
+    for c, (a, b) in enumerate(in_parts):
+        wait_send_all(xs, xr, s1, r1, c, a, b)
+    for c, (a, b) in enumerate(out_parts):
+        wait_send_all(ys, yr, s2, r2, c, a, b)
+
+
+def fused(n, latent, ln_gain, q_gain, k_gain, w_qkv, w_out):
+    rows, columns, model = latent.shape
+    tokens = rows * columns
+    per = tokens // n
+    vmem = pl.BlockSpec(memory_space=pltpu.VMEM)
+    hbm = pl.BlockSpec(memory_space=pl.ANY)
+    block = pltpu.VMEM((n, per, model), BF16)
+    ins, outs = len(IN_CUTS) - 1, len(OUT_CUTS) - 1
+    return pl.pallas_call(
+        functools.partial(kernel, n),
+        out_shape=jax.ShapeDtypeStruct(latent.shape, BF16),
+        in_specs=[vmem, vmem, vmem, vmem, hbm, hbm],
+        out_specs=vmem,
+        scratch_shapes=[
+            block,
+            block,
+            block,
+            block,
+            pltpu.VMEM(w_qkv.shape, BF16),
+            pltpu.VMEM(w_out.shape, BF16),
+            pltpu.VMEM((tokens, w_qkv.shape[1]), F32),
+            pltpu.VMEM((tokens, model), BF16),
+            pltpu.VMEM((tokens, model), BF16),
+            pltpu.VMEM((tokens, model), BF16),
+            pltpu.SemaphoreType.DMA((ins,)),
+            pltpu.SemaphoreType.DMA,
+            pltpu.SemaphoreType.DMA((ins, n)),
+            pltpu.SemaphoreType.DMA((ins, n)),
+            pltpu.SemaphoreType.DMA((outs, n)),
+            pltpu.SemaphoreType.DMA((outs, n)),
+        ],
+        compiler_params=pltpu.CompilerParams(
+            collective_id=0, has_side_effects=True, vmem_limit_bytes=60 * 2**20
+        ),
+    )(
+        latent,
+        ln_gain.reshape(1, -1),
+        q_gain.reshape(1, -1),
+        k_gain.reshape(1, -1),
+        w_qkv,
+        w_out,
+    )
 
 
 def layer_norm(rows, ln_gain):
@@ -50,6 +310,8 @@
     rows, columns, model = latent.shape
     positions = rows * columns
     per_peer = positions // device_count
+    if per_peer % 8 == 0:
+        return fused(device_count, latent, ln_gain, q_gain, k_gain, w_qkv, w_out)
     flat = latent.reshape(positions, model)
     normed = layer_norm(flat, ln_gain)
     query, keys, values = project(

time: 64.5 us -> 32.9 us (0.51)
  blocking collectives: 31.1 us -> 0 us
  Pallas kernels: 0 us -> 29.7 us
  matrix products: 10.8 us -> 0 us
  local copies, waits for them, and re-layouts: 12.5 us -> 2.99 us
  other arithmetic: 9.38 us -> 0 us
    all_to_all x2 -> x0, blocking collectives: 31.1 us -> none  [the longest x1 17.8 us: body(): lax.all_to_all(normed.reshape(device_count, per_peer, model), 'frame', sp...]
    pallas_call x0 -> x1, Pallas kernels: none -> 29.7 us  [fused(): pl.pallas_call(functools.partial(kernel, n), out_shape=jax.ShapeDtypeStru...]
    dot_general x4 -> x0, matrix products: 10.8 us -> none  [the longest x1 4.61 us: project(): jnp.dot(normed.reshape(-1, width), w_qkv, preferred_element_type=jnp.floa...]
    reshape x4 -> x1, local copies, waits for them, and re-layouts: 9.22 us -> 1.29 us  [fused(): ln_gain.reshape(1, -1)]
    reduce_sum x4 -> x0, other arithmetic: 5.55 us -> none  [the longest x2 3.14 us: head_norm(): mean_sq = jnp.mean(shaped * shaped, axis=-1, keepdims=True)]
    convert_element_type x3 -> x0, other arithmetic: 3.78 us -> none  [the longest x1 1.92 us: head_norm(): (shaped * lax.rsqrt(mean_sq + 1e-06) * gain).astype(jnp.bfloat16)]
    convert_element_type x1 -> x0, local copies, waits for them, and re-layouts: 1.97 us -> none  [attend(): return mixed.astype(jnp.bfloat16).reshape(query.shape)]
    unnamed x6 -> x1, local copies, waits for them, and re-layouts: 0.01 us -> 1.7 us
where the time goes in v1:
time: 32.9 us; the launch traced here: 32.7 us
  Pallas kernels  29.7 us (90%)
  local copies, waits for them, and re-layouts  2.99 us (9%)
    pallas_call x1, Pallas kernels, fused(): pl.pallas_call(functools.partial(kernel, n), out_shape=jax.ShapeDtypeStru...  29.7 us
    unnamed x1, local copies, waits for them, and re-layouts  1.7 us
    reshape x1, local copies, waits for them, and re-layouts, fused(): ln_gain.reshape(1, -1)  1.29 us

profile of v1, /device:TPU:0, one launch (start us, length us, event | category | flops | bytes accessed | tf_op | source)
XLA Modules:
  0.0 32.7 jit_solution(1210334762885013838)
XLA Ops:
  0.0 1.3 %reshape.9.ln_ref = f32[1,1152]{1,0:T(1,128)} reshape(f32[1152]{0:T(1024)} %param.7) | data formatting | bytes 9216 | tf_op jit(solution)/shard_map/reshape | solution.py:262
  1.3 29.7 %shard_map.64 = bf16[4,32,1152]{2,1,0:T(8,128)(2,1)} custom-call(bf16[4,32,1152]{2,1,0:T(8,128)(2,1)} %lat_ref.1, f32[1,1152]{1,0:T(1,128)} %reshape.9.ln_ref, f32[1,72]{1,0:T(1,128)} %bitcast.2, f32[1,72]{1,0:T(1,128)} %bitcast.3, bf16[1152,3456]{1,0:T(8,128)(2,1)} %wq_hbm.1, bf16[1152,1152]{1,0:T(8,128)(2,1)} %wo_hbm.1), custom_call_target="tpu_custom_call" | custom-call | tf_op jit(solution)/shard_map/pallas_call | solution.py:234
  31.0 1.7 %copy.8 = bf16[4,32,1152]{2,1,0:T(8,128)(2,1)} copy(bf16[4,32,1152]{2,1,0:T(8,128)(2,1)} %shard_map.64) | data formatting | bytes 589824

commit v2 on v1

--- a/solution.py
+++ b/solution.py
@@ -11,29 +11,25 @@
 HEAD_DIM = 72
 LANES = 128
 IN_CUTS = (0, 512, 1024, 1152)
-OUT_CUTS = (0, 256, 768, 1152)
+MID_CUTS = (0, 384, 768, 1152)
+OUT_CUTS = (0, 256, 640, 1152)
+SPAN = 512
+VMEM_BYTES = 66600000
 MESH = pl.DeviceIdType.MESH
 F32 = jnp.float32
 BF16 = jnp.bfloat16
 
 
-def split_dot(values, ones):
-    high = values.astype(BF16)
-    low = (values - high.astype(F32)).astype(BF16)
-    return jnp.dot(high, ones, preferred_element_type=F32) + jnp.dot(
-        low, ones, preferred_element_type=F32
-    )
-
-
 def kernel(
     n,
-    lat_ref,
+    lat_hbm,
     ln_ref,
     qg_ref,
     kg_ref,
     wq_hbm,
     wo_hbm,
     out_ref,
+    lat,
     xs,
     xr,
     ys,
@@ -43,7 +39,7 @@
     acc,
     qn,
     kn,
-    vb,
+    lat_sem,
     wq_sem,
     wo_sem,
     s1,
@@ -51,7 +47,7 @@
     s2,
     r2,
 ):
-    rows, columns, model = lat_ref.shape
+    rows, columns, model = lat_hbm.shape
     tokens = rows * columns
     per = tokens // n
     me = lax.axis_index("frame")
@@ -60,14 +56,22 @@
 
     barrier = pltpu.get_barrier_semaphore()
 
-    def greet(k, _):
+    def offset(i):
+        return n // 2 + (1 - 2 * lax.rem(i, 2)) * ((i + 1) // 2)
+
+    def greet(i, _):
         pl.semaphore_signal(
-            barrier, inc=1, device_id={"frame": lax.rem(me + k, n)}, device_id_type=MESH
+            barrier,
+            inc=1,
+            device_id={"frame": lax.rem(me + offset(i), n)},
+            device_id_type=MESH,
         )
         return 0
 
-    lax.fori_loop(1, n, greet, 0)
-
+    lax.fori_loop(0, n - 1, greet, 0)
+
+    load_lat = pltpu.make_async_copy(lat_hbm, lat, lat_sem)
+    load_lat.start()
     loads = []
     for c, (a, b) in enumerate(in_parts):
         loads.append(
@@ -77,10 +81,11 @@
     load_out = pltpu.make_async_copy(wo_hbm, wo, wo_sem)
     load_out.start()
 
-    values = lat_ref[...].astype(F32).reshape(tokens, model)
+    load_lat.wait()
+    values = lat[...].astype(F32).reshape(tokens, model)
     center = values - jnp.mean(values, axis=-1, keepdims=True)
     spread = jnp.mean(center * center, axis=-1, keepdims=True)
-    normed = center * lax.rsqrt(spread + 1e-06) * ln_ref[...]
+    normed = center * lax.rsqrt(spread + 1e-06) * ln_ref[...].reshape(1, model)
     xs[...] = normed.reshape(n, per, model).astype(BF16)
     xr[pl.ds(me, 1)] = xs[pl.ds(me, 1)]
 
@@ -97,11 +102,12 @@
         )
 
     def send_all(src, dst, send, recv, c, a, b):
-        def one(k, _):
+        def one(i, _):
+            k = offset(i)
             copy(src, dst, send, recv, c, a, b, k, lax.rem(me + k, n), me).start()
             return 0
 
-        lax.fori_loop(1, n, one, 0)
+        lax.fori_loop(0, n - 1, one, 0)
 
     def wait_recv_all(src, dst, send, recv, c, a, b):
         def one(k, _):
@@ -122,13 +128,6 @@
     for c, (a, b) in enumerate(in_parts):
         send_all(xs, xr, s1, r1, c, a, b)
 
-    lane = lax.broadcasted_iota(jnp.int32, (model, LANES), 0)
-    head = lax.broadcasted_iota(jnp.int32, (model, LANES), 1)
-    gather = ((lane >= head * HEAD_DIM) & (lane < (head + 1) * HEAD_DIM)).astype(F32).astype(BF16)
-    head_t = lax.broadcasted_iota(jnp.int32, (LANES, model), 0)
-    lane_t = lax.broadcasted_iota(jnp.int32, (LANES, model), 1)
-    inside = (lane_t >= head_t * HEAD_DIM) & (lane_t < (head_t + 1) * HEAD_DIM)
-    spread_t = inside.astype(F32).astype(BF16)
     entry = lax.broadcasted_iota(jnp.int32, (HEAD_DIM, model), 0)
     place = lax.broadcasted_iota(jnp.int32, (HEAD_DIM, model), 1)
     picked = entry == place
@@ -137,7 +136,7 @@
     repeat = picked.astype(F32)
 
     def whole_gain(ref):
-        rows8 = jnp.broadcast_to(ref[...], (8, HEAD_DIM))
+        rows8 = jnp.broadcast_to(ref[...].reshape(1, HEAD_DIM), (8, HEAD_DIM))
         return jnp.dot(
             rows8, repeat, preferred_element_type=F32, precision=lax.Precision.HIGHEST
         )[0:1]
@@ -145,12 +144,19 @@
     q_gain = whole_gain(qg_ref)
     k_gain = whole_gain(kg_ref)
 
+    row_i = lax.broadcasted_iota(jnp.int32, (tokens, tokens), 0)
+    col_i = lax.broadcasted_iota(jnp.int32, (tokens, tokens), 1)
+    same = lax.rem(row_i, per) == lax.rem(col_i, per)
+
+    def arrived(c, a, b):
+        wait_recv_all(xs, xr, s1, r1, c, a, b)
+        loads[c].wait()
+        return xr[:, :, a:b].astype(F32).reshape(tokens, b - a).astype(BF16)
+
     width = 3 * model
     step = model // 3
-    for c, (a, b) in enumerate(in_parts):
-        wait_recv_all(xs, xr, s1, r1, c, a, b)
-        loads[c].wait()
-        part = xr[:, :, a:b].astype(F32).reshape(tokens, b - a).astype(BF16)
+    for c, (a, b) in enumerate(in_parts[:-1]):
+        part = arrived(c, a, b)
         for col in range(0, width, step):
             product = jnp.dot(part, wq[a:b, col : col + step], preferred_element_type=F32)
             if c == 0:
@@ -158,45 +164,72 @@
             else:
                 acc[:, col : col + step] += product
 
-    def head_norm(block, gain):
-        sums = split_dot(block * block, gather)
-        scale = lax.rsqrt(sums * (1.0 / HEAD_DIM) + 1e-06)
-        return (block * split_dot(scale, spread_t) * gain).astype(BF16)
-
-    qn[...] = head_norm(acc[:, :model], q_gain)
-    kn[...] = head_norm(acc[:, model : 2 * model], k_gain)
-    vb[...] = acc[:, 2 * model :].astype(BF16)
-
-    row_i = lax.broadcasted_iota(jnp.int32, (tokens, tokens), 0)
-    col_i = lax.broadcasted_iota(jnp.int32, (tokens, tokens), 1)
-    same = lax.rem(row_i, per) == lax.rem(col_i, per)
+    last, (a_in, b_in) = len(in_parts) - 1, in_parts[-1]
+    part = arrived(last, a_in, b_in)
 
     def head_mask(h, lo, hi):
         at = lax.broadcasted_iota(jnp.int32, (tokens, hi - lo), 1) + lo
         return (at >= h * HEAD_DIM) & (at < (h + 1) * HEAD_DIM)
 
     probs = {}
-
-    def attend(h):
-        lo = h * HEAD_DIM // LANES * LANES
-        hi = -(-(h + 1) * HEAD_DIM // LANES) * LANES
-        mask = head_mask(h, lo, hi)
-        query = jnp.where(mask, qn[:, lo:hi].astype(F32), 0.0).astype(BF16)
-        scores = lax.dot_general(
-            query, kn[:, lo:hi], (((1,), (1,)), ((), ())), preferred_element_type=F32
-        ) * (HEAD_DIM**-0.5)
-        weights = jnp.where(same, jnp.exp(scores), 0.0)
-        total = jnp.sum(weights, axis=-1, keepdims=True)
-        probs[h] = (weights * (1.0 / total)).astype(BF16)
-
+    done = 0
     for c, (a, b) in enumerate(out_parts):
+        piece = slice(MID_CUTS[c], MID_CUTS[c + 1])
+        for third in range(3):
+            cols = slice(third * model + piece.start, third * model + piece.stop)
+            acc[:, cols] += jnp.dot(part, wq[a_in:b_in, cols], preferred_element_type=F32)
+
+        first, done = done, piece.stop // HEAD_DIM
+        count = done - first
+        lo = first * HEAD_DIM // LANES * LANES
+        hi = -(-done * HEAD_DIM // LANES) * LANES
+        span = hi - lo
+        lane = lax.broadcasted_iota(jnp.int32, (span, LANES), 0) + lo
+        head = lax.broadcasted_iota(jnp.int32, (span, LANES), 1)
+        start = (head + first) * HEAD_DIM
+        gather = ((head < count) & (lane >= start) & (lane < start + HEAD_DIM)).astype(F32)
+        gather = gather.astype(BF16)
+        head = lax.rem(lax.broadcasted_iota(jnp.int32, (2 * LANES, span), 0), LANES)
+        lane = lax.broadcasted_iota(jnp.int32, (2 * LANES, span), 1) + lo
+        start = (head + first) * HEAD_DIM
+        expand = ((head < count) & (lane >= start) & (lane < start + HEAD_DIM)).astype(F32)
+        expand = expand.astype(BF16)
+
+        def head_norm(base, gain):
+            block = acc[:, base + lo : base + hi]
+            sums = jnp.dot((block * block).astype(BF16), gather, preferred_element_type=F32)
+            scale = lax.rsqrt(sums * (1.0 / HEAD_DIM) + 1e-06)
+            high = scale.astype(BF16)
+            low = (scale - high.astype(F32)).astype(BF16)
+            scale = jnp.dot(
+                jnp.concatenate([high, low], axis=1), expand, preferred_element_type=F32
+            )
+            return (block * scale * gain[:, lo:hi]).astype(BF16)
+
+        qn[:, :span] = head_norm(0, q_gain)
+        kn[:, :span] = head_norm(model, k_gain)
+
+        for h in range(first, done):
+            at = h * HEAD_DIM // LANES * LANES
+            end = -(-(h + 1) * HEAD_DIM // LANES) * LANES
+            mask = head_mask(h, at, end)
+            query = jnp.where(mask, qn[:, at - lo : end - lo].astype(F32), 0.0).astype(BF16)
+            scores = lax.dot_general(
+                query,
+                kn[:, at - lo : end - lo],
+                (((1,), (1,)), ((), ())),
+                preferred_element_type=F32,
+            ) * (HEAD_DIM**-0.5)
+            weights = jnp.where(same, jnp.exp(scores), 0.0)
+            total = jnp.sum(weights, axis=-1, keepdims=True)
+            probs[h] = (weights * (1.0 / total)).astype(BF16)
+
         for tile in range(a, b, LANES):
             out_tile = None
             for h in range(tile // HEAD_DIM, (tile + LANES - 1) // HEAD_DIM + 1):
-                if h not in probs:
-                    attend(h)
                 mask = head_mask(h, tile, tile + LANES)
-                value = jnp.where(mask, vb[:, tile : tile + LANES].astype(F32), 0.0).astype(BF16)
+                value = acc[:, 2 * model + tile : 2 * model + tile + LANES]
+                value = jnp.where(mask, value, 0.0).astype(BF16)
                 term = jnp.dot(probs[h], value, preferred_element_type=F32)
                 out_tile = term if out_tile is None else out_tile + term
             ys[:, :, tile : tile + LANES] = out_tile.reshape(n, per, LANES).astype(BF16)
@@ -204,7 +237,8 @@
     yr[pl.ds(me, 1)] = ys[pl.ds(me, 1)]
 
     load_out.wait()
-    branch = lat_ref[...].astype(F32).reshape(tokens, model)
+    for c, (a, b) in enumerate(in_parts):
+        wait_send_all(xs, xr, s1, r1, c, a, b)
     for c, (a, b) in enumerate(out_parts):
         wait_recv_all(ys, yr, s2, r2, c, a, b)
         part = yr[:, :, a:b].astype(F32).reshape(tokens, b - a).astype(BF16)
@@ -214,11 +248,9 @@
         elif c < len(out_parts) - 1:
             acc[:, :model] += product
         else:
+            branch = lat[...].astype(F32).reshape(tokens, model)
             product = acc[:, :model] + product
             out_ref[...] = (branch + product).reshape(rows, columns, model).astype(BF16)
-
-    for c, (a, b) in enumerate(in_parts):
-        wait_send_all(xs, xr, s1, r1, c, a, b)
     for c, (a, b) in enumerate(out_parts):
         wait_send_all(ys, yr, s2, r2, c, a, b)
 
@@ -228,15 +260,16 @@
     tokens = rows * columns
     per = tokens // n
     vmem = pl.BlockSpec(memory_space=pltpu.VMEM)
-    hbm = pl.BlockSpec(memory_space=pl.ANY)
+    hbm = pl.BlockSpec(memory_space=pltpu.HBM)
     block = pltpu.VMEM((n, per, model), BF16)
     ins, outs = len(IN_CUTS) - 1, len(OUT_CUTS) - 1
     return pl.pallas_call(
         functools.partial(kernel, n),
         out_shape=jax.ShapeDtypeStruct(latent.shape, BF16),
-        in_specs=[vmem, vmem, vmem, vmem, hbm, hbm],
+        in_specs=[hbm, vmem, vmem, vmem, hbm, hbm],
         out_specs=vmem,
         scratch_shapes=[
+            pltpu.VMEM(latent.shape, BF16),
             block,
             block,
             block,
@@ -244,9 +277,9 @@
             pltpu.VMEM(w_qkv.shape, BF16),
             pltpu.VMEM(w_out.shape, BF16),
             pltpu.VMEM((tokens, w_qkv.shape[1]), F32),
-            pltpu.VMEM((tokens, model), BF16),
-            pltpu.VMEM((tokens, model), BF16),
-            pltpu.VMEM((tokens, model), BF16),
+            pltpu.VMEM((tokens, SPAN), BF16),
+            pltpu.VMEM((tokens, SPAN), BF16),
+            pltpu.SemaphoreType.DMA,
             pltpu.SemaphoreType.DMA((ins,)),
             pltpu.SemaphoreType.DMA,
             pltpu.SemaphoreType.DMA((ins, n)),
@@ -255,16 +288,9 @@
             pltpu.SemaphoreType.DMA((outs, n)),
         ],
         compiler_params=pltpu.CompilerParams(
-            collective_id=0, has_side_effects=True, vmem_limit_bytes=60 * 2**20
+            collective_id=0, has_side_effects=True, vmem_limit_bytes=VMEM_BYTES
         ),
-    )(
-        latent,
-        ln_gain.reshape(1, -1),
-        q_gain.reshape(1, -1),
-        k_gain.reshape(1, -1),
-        w_qkv,
-        w_out,
-    )
+    )(latent, ln_gain, q_gain, k_gain, w_qkv, w_out)
 
 
 def layer_norm(rows, ln_gain):

time: 32.9 us -> 30.6 us (0.930)
  local copies, waits for them, and re-layouts: 2.99 us -> 1.7 us
  Pallas kernels: 29.7 us -> 28.8 us
    reshape x1 -> x0, local copies, waits for them, and re-layouts: 1.29 us -> none  [fused(): ln_gain.reshape(1, -1)]
    pallas_call x1, Pallas kernels: 29.7 us -> 28.8 us  [fused(): pl.pallas_call(functools.partial(kernel, n), out_shape=jax.ShapeDtypeStru...]
where the time goes in v2:
time: 30.6 us; the launch traced here: 30.5 us
  Pallas kernels  28.8 us (94%)
  local copies, waits for them, and re-layouts  1.7 us (6%)
    pallas_call x1, Pallas kernels, fused(): pl.pallas_call(functools.partial(kernel, n), out_shape=jax.ShapeDtypeStru...  28.8 us
    unnamed x1, local copies, waits for them, and re-layouts  1.7 us

profile of v2, /device:TPU:0, one launch (start us, length us, event | category | flops | bytes accessed | tf_op | source)
XLA Modules:
  0.0 30.5 jit_solution(15332423823868703951)
XLA Ops:
  0.0 28.8 %shard_map.64 = bf16[4,32,1152]{2,1,0:T(8,128)(2,1)} custom-call(bf16[4,32,1152]{2,1,0:T(8,128)(2,1)} %lat_hbm.1, f32[1152]{0:T(1024)} %ln_ref.1, f32[72]{0:T(128)} %qg_ref.1, f32[72]{0:T(128)} %kg_ref.1, bf16[1152,3456]{1,0:T(8,128)(2,1)} %wq_hbm.1, bf16[1152,1152]{1,0:T(8,128)(2,1)} %wo_hbm.1), custom_call_target="tpu_custom_call" | custom-call | tf_op jit(solution)/shard_map/pallas_call | solution.py:266
  28.8 1.7 %copy.8 = bf16[4,32,1152]{2,1,0:T(8,128)(2,1)} copy(bf16[4,32,1152]{2,1,0:T(8,128)(2,1)} %shard_map.64) | data formatting | bytes 589824

commit v3 on v2

--- a/solution.py
+++ b/solution.py
@@ -14,7 +14,7 @@
 MID_CUTS = (0, 384, 768, 1152)
 OUT_CUTS = (0, 256, 640, 1152)
 SPAN = 512
-VMEM_BYTES = 66600000
+VMEM_BYTES = 30000000
 MESH = pl.DeviceIdType.MESH
 F32 = jnp.float32
 BF16 = jnp.bfloat16
@@ -23,13 +23,16 @@
 def kernel(
     n,
     lat_hbm,
-    ln_ref,
-    qg_ref,
-    kg_ref,
+    ln_hbm,
+    qg_hbm,
+    kg_hbm,
     wq_hbm,
     wo_hbm,
     out_ref,
     lat,
+    ln_ref,
+    qg_ref,
+    kg_ref,
     xs,
     xr,
     ys,
@@ -40,6 +43,7 @@
     qn,
     kn,
     lat_sem,
+    gain_sem,
     wq_sem,
     wo_sem,
     s1,
@@ -72,6 +76,12 @@
 
     load_lat = pltpu.make_async_copy(lat_hbm, lat, lat_sem)
     load_lat.start()
+    gains = [
+        pltpu.make_async_copy(src, dst, gain_sem.at[i])
+        for i, (src, dst) in enumerate(((ln_hbm, ln_ref), (qg_hbm, qg_ref), (kg_hbm, kg_ref)))
+    ]
+    for load in gains:
+        load.start()
     loads = []
     for c, (a, b) in enumerate(in_parts):
         loads.append(
@@ -82,6 +92,8 @@
     load_out.start()
 
     load_lat.wait()
+    for load in gains:
+        load.wait()
     values = lat[...].astype(F32).reshape(tokens, model)
     center = values - jnp.mean(values, axis=-1, keepdims=True)
     spread = jnp.mean(center * center, axis=-1, keepdims=True)
@@ -197,7 +209,11 @@
 
         def head_norm(base, gain):
             block = acc[:, base + lo : base + hi]
-            sums = jnp.dot((block * block).astype(BF16), gather, preferred_element_type=F32)
+            square = block * block
+            high = square.astype(BF16)
+            low = (square - high.astype(F32)).astype(BF16)
+            sums = jnp.dot(high, gather, preferred_element_type=F32)
+            sums += jnp.dot(low, gather, preferred_element_type=F32)
             scale = lax.rsqrt(sums * (1.0 / HEAD_DIM) + 1e-06)
             high = scale.astype(BF16)
             low = (scale - high.astype(F32)).astype(BF16)
@@ -266,10 +282,13 @@
     return pl.pallas_call(
         functools.partial(kernel, n),
         out_shape=jax.ShapeDtypeStruct(latent.shape, BF16),
-        in_specs=[hbm, vmem, vmem, vmem, hbm, hbm],
+        in_specs=[hbm] * 6,
         out_specs=vmem,
         scratch_shapes=[
             pltpu.VMEM(latent.shape, BF16),
+            pltpu.VMEM(ln_gain.shape, F32),
+            pltpu.VMEM(q_gain.shape, F32),
+            pltpu.VMEM(k_gain.shape, F32),
             block,
             block,
             block,
@@ -280,6 +299,7 @@
             pltpu.VMEM((tokens, SPAN), BF16),
             pltpu.VMEM((tokens, SPAN), BF16),
             pltpu.SemaphoreType.DMA,
+            pltpu.SemaphoreType.DMA((3,)),
             pltpu.SemaphoreType.DMA((ins,)),
             pltpu.SemaphoreType.DMA,
             pltpu.SemaphoreType.DMA((ins, n)),
@@ -290,7 +310,12 @@
         compiler_params=pltpu.CompilerParams(
             collective_id=0, has_side_effects=True, vmem_limit_bytes=VMEM_BYTES
         ),
-    )(latent, ln_gain, q_gain, k_gain, w_qkv, w_out)
+    )(
+        *(
+            pltpu.with_memory_space_constraint(value, pltpu.HBM)
+            for value in (latent, ln_gain, q_gain, k_gain, w_qkv, w_out)
+        )
+    )
 
 
 def layer_norm(rows, ln_gain):

time: 30.6 us -> 28.3 us (0.925)
  Pallas kernels: 28.8 us -> 27.5 us
  local copies, waits for them, and re-layouts: 1.7 us -> 0.72 us
    pallas_call x1, Pallas kernels: 28.8 us -> 27.5 us  [fused(): pl.pallas_call(functools.partial(kernel, n), out_shape=jax.ShapeDtypeStru...]
    unnamed x1, local copies, waits for them, and re-layouts: 1.7 us -> 0.72 us
where the time goes in v3:
time: 28.3 us; the launch traced here: 28.2 us
  Pallas kernels  27.5 us (97%)
  local copies, waits for them, and re-layouts  0.72 us (3%)
    pallas_call x1, Pallas kernels, fused(): pl.pallas_call(functools.partial(kernel, n), out_shape=jax.ShapeDtypeStru...  27.5 us
    unnamed x1, local copies, waits for them, and re-layouts  0.72 us

profile of v3, /device:TPU:0, one launch (start us, length us, event | category | flops | bytes accessed | tf_op | source)
XLA Modules:
  0.0 28.2 jit_solution(12440894887238933211)
XLA Ops:
  0.0 27.5 %shard_map.64 = bf16[4,32,1152]{2,1,0:T(8,128)(2,1)S(1)} custom-call(bf16[4,32,1152]{2,1,0:T(8,128)(2,1)} %lat_hbm.1, f32[1152]{0:T(1024)} %ln_hbm.1, f32[72]{0:T(128)} %qg_hbm.1, f32[72]{0:T(128)} %kg_hbm.1, bf16[1152,3456]{1,0:T(8,128)(2,1)} %wq_hbm.1, bf16[1152,1152]{1,0:T(8,128)(2,1)} %wo_hbm.1), custom_call_target="tpu_custom_call" | custom-call | tf_op jit(solution)/shard_map/pallas_call | solution.py:282
  27.5 0.7 %copy.8 = bf16[4,32,1152]{2,1,0:T(8,128)(2,1)} copy(bf16[4,32,1152]{2,1,0:T(8,128)(2,1)S(1)} %shard_map.64) | data formatting | bytes 589824

commit v4 on v3

--- a/solution.py
+++ b/solution.py
@@ -10,7 +10,7 @@
 HEADS = 16
 HEAD_DIM = 72
 LANES = 128
-IN_CUTS = (0, 512, 1024, 1152)
+IN_CUTS = (0, 640, 1152)
 MID_CUTS = (0, 384, 768, 1152)
 OUT_CUTS = (0, 256, 640, 1152)
 SPAN = 512
@@ -60,19 +60,10 @@
 
     barrier = pltpu.get_barrier_semaphore()
 
-    def offset(i):
-        return n // 2 + (1 - 2 * lax.rem(i, 2)) * ((i + 1) // 2)
-
-    def greet(i, _):
-        pl.semaphore_signal(
-            barrier,
-            inc=1,
-            device_id={"frame": lax.rem(me + offset(i), n)},
-            device_id_type=MESH,
-        )
-        return 0
-
-    lax.fori_loop(0, n - 1, greet, 0)
+    steps = sorted(range(1, n), key=lambda k: (abs(k - n // 2), k))
+    peers = [lax.rem(me + k, n) for k in steps]
+    for to in peers:
+        pl.semaphore_signal(barrier, inc=1, device_id={"frame": to}, device_id_type=MESH)
 
     load_lat = pltpu.make_async_copy(lat_hbm, lat, lat_sem)
     load_lat.start()
@@ -103,39 +94,32 @@
 
     pl.semaphore_wait(barrier, n - 1)
 
-    def copy(src, dst, send, recv, c, a, b, k, to, slot):
+    def send_all(src, dst, send, recv, c, a, b):
+        for to in peers:
+            pltpu.make_async_remote_copy(
+                src_ref=src.at[to, :, pl.ds(a, b - a)],
+                dst_ref=dst.at[me, :, pl.ds(a, b - a)],
+                send_sem=send.at[c],
+                recv_sem=recv.at[c],
+                device_id={"frame": to},
+                device_id_type=MESH,
+            ).start()
+
+    def all_copies(src, dst, send, recv, c, a, b):
         return pltpu.make_async_remote_copy(
-            src_ref=src.at[to, :, pl.ds(a, b - a)],
-            dst_ref=dst.at[slot, :, pl.ds(a, b - a)],
-            send_sem=send.at[c, k],
-            recv_sem=recv.at[c, k],
-            device_id={"frame": to},
+            src_ref=src.at[pl.ds(0, n - 1), :, pl.ds(a, b - a)],
+            dst_ref=dst.at[pl.ds(0, n - 1), :, pl.ds(a, b - a)],
+            send_sem=send.at[c],
+            recv_sem=recv.at[c],
+            device_id={"frame": peers[0]},
             device_id_type=MESH,
         )
 
-    def send_all(src, dst, send, recv, c, a, b):
-        def one(i, _):
-            k = offset(i)
-            copy(src, dst, send, recv, c, a, b, k, lax.rem(me + k, n), me).start()
-            return 0
-
-        lax.fori_loop(0, n - 1, one, 0)
-
     def wait_recv_all(src, dst, send, recv, c, a, b):
-        def one(k, _):
-            copy(
-                src, dst, send, recv, c, a, b, k, lax.rem(me + k, n), lax.rem(me + n - k, n)
-            ).wait_recv()
-            return 0
-
-        lax.fori_loop(1, n, one, 0)
+        all_copies(src, dst, send, recv, c, a, b).wait_recv()
 
     def wait_send_all(src, dst, send, recv, c, a, b):
-        def one(k, _):
-            copy(src, dst, send, recv, c, a, b, k, lax.rem(me + k, n), me).wait_send()
-            return 0
-
-        lax.fori_loop(1, n, one, 0)
+        all_copies(src, dst, send, recv, c, a, b).wait_send()
 
     for c, (a, b) in enumerate(in_parts):
         send_all(xs, xr, s1, r1, c, a, b)
@@ -302,10 +286,10 @@
             pltpu.SemaphoreType.DMA((3,)),
             pltpu.SemaphoreType.DMA((ins,)),
             pltpu.SemaphoreType.DMA,
-            pltpu.SemaphoreType.DMA((ins, n)),
-            pltpu.SemaphoreType.DMA((ins, n)),
-            pltpu.SemaphoreType.DMA((outs, n)),
-            pltpu.SemaphoreType.DMA((outs, n)),
+            pltpu.SemaphoreType.DMA((ins,)),
+            pltpu.SemaphoreType.DMA((ins,)),
+            pltpu.SemaphoreType.DMA((outs,)),
+            pltpu.SemaphoreType.DMA((outs,)),
         ],
         compiler_params=pltpu.CompilerParams(
             collective_id=0, has_side_effects=True, vmem_limit_bytes=VMEM_BYTES

time: 28.3 us -> 25.7 us (0.908)
  Pallas kernels: 27.5 us -> 24.8 us
    pallas_call x1, Pallas kernels: 27.5 us -> 24.8 us  [fused(): pl.pallas_call(functools.partial(kernel, n), out_shape=jax.ShapeDtypeStru...]
where the time goes in v4:
time: 25.7 us; the launch traced here: 25.6 us
  Pallas kernels  24.8 us (96%)
  local copies, waits for them, and re-layouts  0.72 us (3%)
    pallas_call x1, Pallas kernels, fused(): pl.pallas_call(functools.partial(kernel, n), out_shape=jax.ShapeDtypeStru...  24.8 us
    unnamed x1, local copies, waits for them, and re-layouts  0.72 us

profile of v4, /device:TPU:0, one launch (start us, length us, event | category | flops | bytes accessed | tf_op | source)
XLA Modules:
  0.0 25.6 jit_solution(11436753944850533968)
XLA Ops:
  0.0 24.8 %shard_map.64 = bf16[4,32,1152]{2,1,0:T(8,128)(2,1)S(1)} custom-call(bf16[4,32,1152]{2,1,0:T(8,128)(2,1)} %lat_hbm.1, f32[1152]{0:T(1024)} %ln_hbm.1, f32[72]{0:T(128)} %qg_hbm.1, f32[72]{0:T(128)} %kg_hbm.1, bf16[1152,3456]{1,0:T(8,128)(2,1)} %wq_hbm.1, bf16[1152,1152]{1,0:T(8,128)(2,1)} %wo_hbm.1), custom_call_target="tpu_custom_call" | custom-call | tf_op jit(solution)/shard_map/pallas_call | solution.py:266
  24.8 0.7 %copy.8 = bf16[4,32,1152]{2,1,0:T(8,128)(2,1)} copy(bf16[4,32,1152]{2,1,0:T(8,128)(2,1)S(1)} %shard_map.64) | data formatting | bytes 589824

commit v5 on v4

--- a/solution.py
+++ b/solution.py
@@ -10,7 +10,7 @@
 HEADS = 16
 HEAD_DIM = 72
 LANES = 128
-IN_CUTS = (0, 640, 1152)
+IN_CUTS = (0, 1152)
 MID_CUTS = (0, 384, 768, 1152)
 OUT_CUTS = (0, 256, 640, 1152)
 SPAN = 512
@@ -60,7 +60,7 @@
 
     barrier = pltpu.get_barrier_semaphore()
 
-    steps = sorted(range(1, n), key=lambda k: (abs(k - n // 2), k))
+    steps = range(1, n)
     peers = [lax.rem(me + k, n) for k in steps]
     for to in peers:
         pl.semaphore_signal(barrier, inc=1, device_id={"frame": to}, device_id_type=MESH)
@@ -173,7 +173,8 @@
         piece = slice(MID_CUTS[c], MID_CUTS[c + 1])
         for third in range(3):
             cols = slice(third * model + piece.start, third * model + piece.stop)
-            acc[:, cols] += jnp.dot(part, wq[a_in:b_in, cols], preferred_element_type=F32)
+            product = jnp.dot(part, wq[a_in:b_in, cols], preferred_element_type=F32)
+            acc[:, cols] = product if last == 0 else acc[:, cols] + product
 
         first, done = done, piece.stop // HEAD_DIM
         count = done - first

time: 25.7 us -> 25 us (0.973)
  Pallas kernels: 24.8 us -> 24.1 us
    pallas_call x1, Pallas kernels: 24.8 us -> 24.1 us  [fused(): pl.pallas_call(functools.partial(kernel, n), out_shape=jax.ShapeDtypeStru...]
where the time goes in v5:
time: 25 us; the launch traced here: 24.8 us
  Pallas kernels  24.1 us (96%)
  local copies, waits for them, and re-layouts  0.72 us (3%)
    pallas_call x1, Pallas kernels, fused(): pl.pallas_call(functools.partial(kernel, n), out_shape=jax.ShapeDtypeStru...  24.1 us
    unnamed x1, local copies, waits for them, and re-layouts  0.72 us

profile of v5, /device:TPU:0, one launch (start us, length us, event | category | flops | bytes accessed | tf_op | source)
XLA Modules:
  0.0 24.8 jit_solution(3997169283391227115)
XLA Ops:
  0.0 24.1 %shard_map.64 = bf16[4,32,1152]{2,1,0:T(8,128)(2,1)S(1)} custom-call(bf16[4,32,1152]{2,1,0:T(8,128)(2,1)} %lat_hbm.1, f32[1152]{0:T(1024)} %ln_hbm.1, f32[72]{0:T(128)} %qg_hbm.1, f32[72]{0:T(128)} %kg_hbm.1, bf16[1152,3456]{1,0:T(8,128)(2,1)} %wq_hbm.1, bf16[1152,1152]{1,0:T(8,128)(2,1)} %wo_hbm.1), custom_call_target="tpu_custom_call" | custom-call | tf_op jit(solution)/shard_map/pallas_call | solution.py:267
  24.1 0.7 %copy.8 = bf16[4,32,1152]{2,1,0:T(8,128)(2,1)} copy(bf16[4,32,1152]{2,1,0:T(8,128)(2,1)S(1)} %shard_map.64) | data formatting | bytes 589824
